TPU v7x, 256 devices: a whole 4x4x8 slice. The times are simulated.
256 devices in a mesh: dp: 32 (over y, x, core), filter: 8 (over z).
Axes of the slice: x: 4, y: 4, z: 8, core: 2. Of those that a mesh axis runs over, the one named last changes fastest.
Arguments:
- inputs: bfloat16 [32, 48, 24, 1024], P('dp', None, None, 'filter'), may hold values from -6 to 6
- kernel: bfloat16 [3, 3, 1024, 1024], P(None, None, 'filter'), may hold values from -0.0625 to 0.0625
- cotangent: bfloat16 [32, 48, 24, 1024], P('dp', 'filter'), may hold values from -6 to 6
Outputs:
- outputs: bfloat16 [32, 48, 24, 1024], P('dp', 'filter')
- input_grad: bfloat16 [32, 48, 24, 1024], P('dp', None, None, 'filter')
- kernel_grad: float32 [1024, 3, 3, 1024], P('dp', None, None, 'filter')
All inputs are finite; a program needn't handle non-finite values.
Results may differ from a plain program's by a relative error of at most 0.001.
Values may be sent and summed in bfloat16 or wider, within the bound.
No kernel may reach another device: no remote copies, remote signals or barrier semaphores. Data moves between devices by JAX's collectives and lax.ppermute only.
A program may use at most 128 MiB of HBM per device.

v0:
```python
import jax
import jax.numpy as jnp
from jax import lax
from jax.sharding import PartitionSpec as P


def conv_rows(xpad, weights, count, width):
    total = jnp.zeros((count, width, weights.shape[3]), jnp.float32)
    for a in range(3):
        for b in range(3):
            total = total + jnp.einsum(
                "hwi,io->hwo",
                xpad[a : a + count, b : b + width],
                weights[a, b],
                preferred_element_type=jnp.float32,
            )
    return total


def on_device(inputs, kernel, cotangent):
    sample = inputs[0]
    height = sample.shape[0]
    width = sample.shape[1]
    local_in = sample.shape[2]
    channels = kernel.shape[3]
    groups = lax.axis_size("filter")
    my_rows = height // groups
    xpad = jnp.pad(sample, ((1, 1), (1, 1), (0, 0)))
    summed = lax.psum_scatter(
        conv_rows(xpad, kernel, my_rows * lax.axis_size("filter"), width),
        "filter",
        scatter_dimension=0,
        tiled=True,
    )
    outputs = summed.astype(jnp.bfloat16)[None]
    start = jnp.int32(0)
    back_pad = jnp.zeros((height + 2, width + 2, local_in), jnp.float32)
    grad_rows = lax.all_gather(cotangent, "filter", axis=1, tiled=True)[0]
    count = grad_rows.shape[0]
    taps = []
    for a in range(3):
        for b in range(3):
            contrib = jnp.einsum(
                "hwo,io->hwi", grad_rows, kernel[a, b], preferred_element_type=jnp.float32
            )
            region = lax.dynamic_slice(back_pad, (start + a, b, 0), (count, width, local_in))
            back_pad = lax.dynamic_update_slice(back_pad, region + contrib, (start + a, b, 0))
            taps.append(
                jnp.einsum(
                    "hwi,hwo->oi",
                    xpad[a : a + count, b : b + width],
                    grad_rows,
                    preferred_element_type=jnp.float32,
                )
            )
    grads = jnp.stack(taps, 1).reshape(channels, 3, 3, local_in)
    back_pad, grads = (back_pad, grads)
    input_grad = back_pad[1:-1, 1:-1].astype(jnp.bfloat16)[None]
    samples = lax.axis_size("dp")
    scale = 1.0 / jnp.sqrt(jnp.float32(samples * height * width))
    whole = lax.psum(grads, "dp")
    share = channels // samples
    mine = lax.dynamic_slice_in_dim(whole, lax.axis_index("dp") * share, share, 0)
    return (outputs, input_grad, mine * scale)


def solution(mesh):
    return jax.shard_map(
        on_device,
        mesh=mesh,
        in_specs=(
            P("dp", None, None, "filter"),
            P(None, None, "filter", None),
            P("dp", "filter", None, None),
        ),
        out_specs=(
            P("dp", "filter", None, None),
            P("dp", None, None, "filter"),
            P("dp", None, None, "filter"),
        ),
        check_vma=False,
    )
```

profile of v0, /device:TPU:1, one launch (start us, length us, event | category | flops | bytes accessed | tf_op | source)
XLA Modules:
  0.0 268.3 jit_solution(1624768555959365311)
XLA Ops:
  8.0 4.1 %fusion.124 = f32[48,24,1024]{2,1,0:T(8,128)} fusion(bf16[3,3,128,1024]{3,2,1,0:T(8,128)(2,1)} %param.4, bf16[48,24,128]{2,1,0:T(8,128)(2,1)} %bitcast.236), kind=kOutput, calls=%fused_computation.79 | convolution fusion | flops 301989888 | bytes 5275648 | tf_op jit(solution)/shard_map/hwi,io->hwo/dot_general | solution.py:11
  12.0 3.8 %fusion.127 = f32[48,24,1024]{2,1,0:T(8,128)} fusion(bf16[3,3,128,1024]{3,2,1,0:T(8,128)(2,1)} %param.4, bf16[48,24,128]{2,1,0:T(8,128)(2,1)S(1)} %bitcast.237), kind=kOutput, calls=%fused_computation.82 | convolution fusion | flops 301989888 | bytes 5275648 | tf_op jit(solution)/shard_map/hwi,io->hwo/dot_general | solution.py:11
  15.8 3.9 %fusion.130 = f32[48,24,1024]{2,1,0:T(8,128)} fusion(bf16[3,3,128,1024]{3,2,1,0:T(8,128)(2,1)} %param.4, bf16[48,24,128]{2,1,0:T(8,128)(2,1)S(1)} %bitcast.238), kind=kOutput, calls=%fused_computation.85 | convolution fusion | flops 301989888 | bytes 5275648 | tf_op jit(solution)/shard_map/hwi,io->hwo/dot_general | solution.py:11
  19.8 3.9 %fusion.136 = f32[48,24,1024]{2,1,0:T(8,128)} fusion(bf16[3,3,128,1024]{3,2,1,0:T(8,128)(2,1)} %param.4, bf16[48,24,128]{2,1,0:T(8,128)(2,1)S(1)} %bitcast.239), kind=kOutput, calls=%fused_computation.91 | convolution fusion | flops 301989888 | bytes 5275648 | tf_op jit(solution)/shard_map/hwi,io->hwo/dot_general | solution.py:11
  23.6 3.9 %fusion.139 = f32[48,24,1024]{2,1,0:T(8,128)} fusion(bf16[3,3,128,1024]{3,2,1,0:T(8,128)(2,1)} %param.4, bf16[48,24,128]{2,1,0:T(8,128)(2,1)S(1)} %bitcast.240), kind=kOutput, calls=%fused_computation.94 | convolution fusion | flops 301989888 | bytes 5275648 | tf_op jit(solution)/shard_map/hwi,io->hwo/dot_general | solution.py:11
  27.5 24.7 %all-gather.2.cloned.1.call-done = bf16[1,48,24,1024]{3,2,0,1:T(8,128)(2,1)} async-done(((bf16[1,6,24,1024]{3,2,0,1:T(8,128)(2,1)}), bf16[1,48,24,1024]{3,2,0,1:T(8,128)(2,1)}) %all-gather.2.cloned.1.call-update) | async-done | bytes 2359312 | tf_op jit(solution)/shard_map/all_gather | solution.py:38
  52.3 3.2 %fusion.69 = f32[1024,9,128]{0,2,1:T(8,128)} fusion(bf16[1,48,24,1024]{3,2,0,1:T(8,128)(2,1)} %all-gather.2.cloned.1.call-done, bf16[48,24,128]{2,1,0:T(8,128)(2,1)S(1)} %bitcast.241), kind=kOutput, calls=%fused_computation.48 | convolution fusion | flops 301989888 | bytes 3178496 | tf_op jit(solution)/shard_map/hwi,hwo->oi/dot_general | solution.py:49
  64.9 1.4 fusion.117
  66.3 6.0 %copy.46 = f32[1024,3,3,128]{3,0,2,1:T(8,128)} copy(f32[1024,3,3,128]{0,3,2,1:T(8,128)} %bitcast.58) | data formatting | bytes 9437184 | tf_op jit(solution)/shard_map/reshape | solution.py:56
  72.4 4.2 %fusion.145 = f32[48,24,1024]{2,1,0:T(8,128)} fusion(bf16[3,3,128,1024]{3,2,1,0:T(8,128)(2,1)} %param.4, bf16[48,24,128]{2,1,0:T(8,128)(2,1)S(1)} %bitcast.249), kind=kOutput, calls=%fused_computation.100 | convolution fusion | flops 301989888 | bytes 5275648 | tf_op jit(solution)/shard_map/hwi,io->hwo/dot_general | solution.py:11
  76.6 4.0 %fusion.142 = f32[48,24,1024]{2,1,0:T(8,128)} fusion(bf16[3,3,128,1024]{3,2,1,0:T(8,128)(2,1)} %param.4, bf16[48,24,128]{2,1,0:T(8,128)(2,1)S(1)} %bitcast.250), kind=kOutput, calls=%fused_computation.97 | convolution fusion | flops 301989888 | bytes 5275648 | tf_op jit(solution)/shard_map/hwi,io->hwo/dot_general | solution.py:11
  80.6 3.9 %fusion.133 = f32[48,24,1024]{2,1,0:T(8,128)} fusion(bf16[3,3,128,1024]{3,2,1,0:T(8,128)(2,1)} %param.4, bf16[1,48,24,128]{3,2,1,0:T(8,128)(2,1)S(1)} %copy-done.1), kind=kOutput, calls=%fused_computation.88 | convolution fusion | flops 301989888 | bytes 5275648 | tf_op jit(solution)/shard_map/hwi,io->hwo/dot_general | solution.py:11
  84.6 13.1 %add_add_fusion = f32[48,24,1024]{2,1,0:T(8,128)} fusion(f32[48,24,1024]{2,1,0:T(8,128)S(1)} %bitcast.253, f32[48,24,1024]{2,1,0:T(8,128)S(1)} %bitcast.255, f32[48,24,1024]{2,1,0:T(8,128)} %fusion.130, f32[48,24,1024]{2,1,0:T(8,128)} %fusion.133, f32[48,24,1024]{2,1,0:T(8,128)} %fusion.136, f32[48,24,1024]{2,1,0:T(8,128)} %fusion.139, ...), kind=kOutput, calls=%fused_computation | convolution fusion | flops 311427072 | bytes 43024384 | tf_op jit(solution)/shard_map/hwi,io->hwo/dot_general | solution.py:11
  97.7 1.7 fusion.34
  99.6 2.6 fusion.36
  102.1 6.3 %dynamic_update_slice.28 = f32[50,26,128]{2,1,0:T(8,128)S(1)} dynamic-update-slice(f32[50,26,128]{2,1,0:T(8,128)S(1)} %dynamic_update_slice.27, f32[48,24,128]{2,1,0:T(8,128)} %fusion.36, s32[]{:T(128)} %constant.5.clone.1, s32[]{:T(128)} %constant.6.clone.1, s32[]{:T(128)} %constant.5.clone.1) | dynamic-update-slice | bytes 1179652 | tf_op jit(solution)/shard_map/dynamic_update_slice | solution.py:47
  108.5 2.6 fusion.39
  111.0 6.3 %dynamic_update_slice.29 = f32[50,26,128]{2,1,0:T(8,128)S(1)} dynamic-update-slice(f32[50,26,128]{2,1,0:T(8,128)S(1)} %dynamic_update_slice.28, f32[48,24,128]{2,1,0:T(8,128)} %fusion.39, s32[]{:T(128)} %constant.5.clone.1, s32[]{:T(128)} %constant.7.clone.1, s32[]{:T(128)} %constant.5.clone.1) | dynamic-update-slice | bytes 1179652 | tf_op jit(solution)/shard_map/dynamic_update_slice | solution.py:47
  117.3 1.9 fusion.45
  119.2 2.6 fusion.48
  121.8 6.3 %dynamic_update_slice.31 = f32[50,26,128]{2,1,0:T(8,128)S(1)} dynamic-update-slice(f32[50,26,128]{2,1,0:T(8,128)S(1)} %fusion.45, f32[48,24,128]{2,1,0:T(8,128)} %fusion.48, s32[]{:T(128)} %constant.6.clone.1, s32[]{:T(128)} %constant.6.clone.1, s32[]{:T(128)} %constant.5.clone.1) | dynamic-update-slice | bytes 1179652 | tf_op jit(solution)/shard_map/dynamic_update_slice | solution.py:47
  128.1 2.6 fusion.51
  130.6 6.3 %dynamic_update_slice.32 = f32[50,26,128]{2,1,0:T(8,128)S(1)} dynamic-update-slice(f32[50,26,128]{2,1,0:T(8,128)S(1)} %dynamic_update_slice.31, f32[48,24,128]{2,1,0:T(8,128)} %fusion.51, s32[]{:T(128)} %constant.6.clone.1, s32[]{:T(128)} %constant.7.clone.1, s32[]{:T(128)} %constant.5.clone.1) | dynamic-update-slice | bytes 1179652 | tf_op jit(solution)/shard_map/dynamic_update_slice | solution.py:47
  136.9 1.8 fusion.57
  138.8 2.6 fusion.60
  141.3 6.2 %dynamic_update_slice.34 = f32[50,26,128]{2,1,0:T(8,128)S(1)} dynamic-update-slice(f32[50,26,128]{2,1,0:T(8,128)S(1)} %fusion.57, f32[48,24,128]{2,1,0:T(8,128)} %fusion.60, s32[]{:T(128)} %constant.7.clone.1, s32[]{:T(128)} %constant.6.clone.1, s32[]{:T(128)} %constant.5.clone.1) | dynamic-update-slice | bytes 1179652 | tf_op jit(solution)/shard_map/dynamic_update_slice | solution.py:47
  147.6 2.6 fusion.63
  150.1 6.2 %dynamic_update_slice.35 = f32[50,26,128]{2,1,0:T(8,128)S(1)} dynamic-update-slice(f32[50,26,128]{2,1,0:T(8,128)S(1)} %dynamic_update_slice.34, f32[48,24,128]{2,1,0:T(8,128)} %fusion.63, s32[]{:T(128)} %constant.7.clone.1, s32[]{:T(128)} %constant.7.clone.1, s32[]{:T(128)} %constant.5.clone.1) | dynamic-update-slice | bytes 1179652 | tf_op jit(solution)/shard_map/dynamic_update_slice | solution.py:47
  157.1 40.0 %all-reduce.4.cloned.1.call-done = f32[1024,3,3,128]{3,0,2,1:T(8,128)} async-done(((f32[1024,3,3,128]{3,0,2,1:T(8,128)}), f32[1024,3,3,128]{3,0,2,1:T(8,128)}) %all-reduce.4.cloned.1.call-update) | async-done | bytes 4718608 | tf_op jit(solution)/shard_map/psum | solution.py:61
  197.2 1.6 dynamic-slice_multiply_fusion
  198.8 61.2 %reduce-scatter.2.cloned.1.call-done = f32[6,24,1024]{2,1,0:T(8,128)} async-done(((f32[48,24,1024]{2,1,0:T(8,128)}), f32[6,24,1024]{2,1,0:T(8,128)}) %reduce-scatter.2.cloned.1.call-update) | async-done | bytes 589840 | tf_op jit(solution)/shard_map/reduce_scatter | solution.py:29
  259.9 1.8 convert_bitcast_fusion
  (29 shorter events, 11.2 us)
Async XLA Ops:
  7.2 45.1 %all-gather.2.cloned.1.call-start = ((), (), s32[]{:S(2)}) async-start(), calls=%async_computation.2 | async-start | bytes 2654208 | tf_op jit(solution)/shard_map/all_gather | solution.py:38
  7.9 189.3 %all-reduce.4.cloned.1.call-start = ((), (), s32[]{:S(2)}) async-start(), calls=%async_computation.3 | async-start | bytes 9437184 | tf_op jit(solution)/shard_map/psum | solution.py:61
  7.9 4.1 %copy-start.1 = (bf16[1,48,24,128]{3,2,1,0:T(8,128)(2,1)S(1)}, bf16[1,48,24,128]{3,2,1,0:T(8,128)(2,1)}, u32[]{:S(2)}) copy-start(bf16[1,48,24,128]{3,2,1,0:T(8,128)(2,1)} %param.3) | copy-start | bytes 884740
  52.3 3.2 %copy-start = (bf16[1,48,24,1024]{3,2,0,1:T(8,128)(2,1)S(1)}, bf16[1,48,24,1024]{3,2,0,1:T(8,128)(2,1)}, u32[]{:S(2)}) copy-start(bf16[1,48,24,1024]{3,2,0,1:T(8,128)(2,1)} %all-gather.2.cloned.1.call-done) | copy-start | bytes 7077892
  72.3 187.6 %reduce-scatter.2.cloned.1.call-start = ((), (), s32[]{:S(2)}) async-start(), calls=%async_computation.1 | async-start | bytes 5308416 | tf_op jit(solution)/shard_map/reduce_scatter | solution.py:29
  72.4 12.2 %slice-start = ((s8[4718592]{0:T(1024)(128)(4,1)}), s8[4194304]{0:T(1024)(128)(4,1)S(1)}, s32[]{:S(2)}) async-start(s8[4718592]{0:T(1024)(128)(4,1)} %bitcast.252), calls=%async_computation.4 | async-start | bytes 8388608
  72.4 12.2 %slice-start.2 = ((s8[4718592]{0:T(1024)(128)(4,1)}), s8[4194304]{0:T(1024)(128)(4,1)S(1)}, s32[]{:S(2)}) async-start(s8[4718592]{0:T(1024)(128)(4,1)} %bitcast.254), calls=%async_computation.6 | async-start | bytes 8388608
  76.6 8.0 %slice-start.1 = ((s8[4718592]{0:T(1024)(128)(4,1)}), s8[524288]{0:T(1024)(128)(4,1)S(1)}, s32[]{:S(2)}) async-start(s8[4718592]{0:T(1024)(128)(4,1)} %bitcast.252), calls=%async_computation.5 | async-start | bytes 1048576
  76.6 8.0 %slice-start.3 = ((s8[4718592]{0:T(1024)(128)(4,1)}), s8[524288]{0:T(1024)(128)(4,1)S(1)}, s32[]{:S(2)}) async-start(s8[4718592]{0:T(1024)(128)(4,1)} %bitcast.254), calls=%async_computation.7 | async-start | bytes 1048576
Sparse Core Ops, SparseCore 0:
  9.8 42.4 all-gather.1
  72.5 124.6 all-reduce.3
  199.9 59.9 reduce-scatter.1
where the time goes:
time: 270 us; the launch traced here: 268 us
  waiting for transfers between devices  127 us (47%)
  matrix products  79.7 us (30%)
  local copies, waits for them, and re-layouts  44.6 us (17%)
  between operations  13.9 us (5%)
  other arithmetic  3.4 us (1%)
    reduce_scatter x1, waiting for transfers between devices, on_device(): lax.psum_scatter(conv_rows(xpad, kernel, my_rows * lax.axis_size('filter'...  61.2 us
    dot_general x9, matrix products, conv_rows(): jnp.einsum('hwi,io->hwo', xpad[a:a + count, b:b + width], weights[a, b],...  44.8 us
    psum x1, waiting for transfers between devices, on_device(): whole = lax.psum(grads, 'dp')  40 us
    dynamic_update_slice x7, local copies, waits for them, and re-layouts, on_device(): lax.dynamic_update_slice(back_pad, region + contrib, (start + a, b, 0))  37.7 us
    all_gather x1, waiting for transfers between devices, on_device(): grad_rows = lax.all_gather(cotangent, 'filter', axis=1, tiled=True)[0]  24.7 us
    dot_general x9, matrix products, on_device(): jnp.einsum('hwo,io->hwi', grad_rows, kernel[a, b], preferred_element_type...  20.9 us
    dot_general x9, matrix products, on_device(): jnp.einsum('hwi,hwo->oi', xpad[a:a + count, b:b + width], grad_rows, pref...  14 us
    reshape x1, local copies, waits for them, and re-layouts, on_device(): grads = jnp.stack(taps, 1).reshape(channels, 3, 3, local_in)  6.04 us
  transfers between devices with their start and end apart: 3, of which 3 were waited for; matrix products, arithmetic and copies ran while one was open for 39% of the time, Pallas kernels for 0%

commit v1 on v0

--- a/solution.py
+++ b/solution.py
@@ -2,6 +2,13 @@
 import jax.numpy as jnp
 from jax import lax
 from jax.sharding import PartitionSpec as P
+
+
+def pass_yards_on(vector):
+    inter = jax.lax.axis_size("filter")
+    b_now = jnp.stack([vector] * inter, 0)
+    right_arr = jax.lax.all_to_all(b_now, axis_name="filter", split_axis=0, concat_axis=0)
+    return jnp.concatenate(right_arr, 1)
 
 
 def conv_rows(xpad, weights, count, width):
@@ -35,7 +42,7 @@
     outputs = summed.astype(jnp.bfloat16)[None]
     start = jnp.int32(0)
     back_pad = jnp.zeros((height + 2, width + 2, local_in), jnp.float32)
-    grad_rows = lax.all_gather(cotangent, "filter", axis=1, tiled=True)[0]
+    grad_rows = pass_yards_on(cotangent)[0]
     count = grad_rows.shape[0]
     taps = []
     for a in range(3):

time: 270 us -> 227 us (0.84)
  waiting for transfers between devices: 127 us -> 72.2 us
  starting transfers between devices: 0.12 us -> 9.23 us
    reduce_scatter x1, waiting for transfers between devices: 61.2 us -> 0.01 us  [on_device(): lax.psum_scatter(conv_rows(xpad, kernel, my_rows * lax.axis_size('filter'...]
    all_to_all x0 -> x1, waiting for transfers between devices: none -> 37.8 us  [pass_yards_on(): jax.lax.all_to_all(b_now, axis_name='filter', split_axis=0, concat_axis=0)]
    all_gather x1 -> x0, waiting for transfers between devices: 24.7 us -> none  [on_device(): grad_rows = lax.all_gather(cotangent, 'filter', axis=1, tiled=True)[0]]
    all_to_all x0 -> x1, starting transfers between devices: none -> 9.15 us  [pass_yards_on(): jax.lax.all_to_all(b_now, axis_name='filter', split_axis=0, concat_axis=0)]
    psum x1, waiting for transfers between devices: 40 us -> 34.4 us  [on_device(): whole = lax.psum(grads, 'dp')]
    another operation x0 -> x1, local copies, waits for them, and re-layouts: none -> 2.71 us  [pass_yards_on(): b_now = jnp.stack([vector] * inter, 0)]
  transfers between devices with their start and end apart: 3 -> 3, of which waited for: 3 -> 2; matrix products, arithmetic and copies ran while one was open for 39% -> 47% of each run, Pallas kernels for 0% -> 0%
where the time goes in v1:
time: 227 us; the launch traced here: 226 us
  matrix products  77.8 us (34%)
  waiting for transfers between devices  72.2 us (32%)
  local copies, waits for them, and re-layouts  47.3 us (21%)
  between operations  15.6 us (7%)
  starting transfers between devices  9.23 us (4%)
  other arithmetic  3.4 us (1%)
    dot_general x9, matrix products, conv_rows(): jnp.einsum('hwi,io->hwo', xpad[a:a + count, b:b + width], weights[a, b],...  44.7 us
    all_to_all x1, waiting for transfers between devices, pass_yards_on(): jax.lax.all_to_all(b_now, axis_name='filter', split_axis=0, concat_axis=0)  37.8 us
    dynamic_update_slice x7, local copies, waits for them, and re-layouts, on_device(): lax.dynamic_update_slice(back_pad, region + contrib, (start + a, b, 0))  37.8 us
    psum x1, waiting for transfers between devices, on_device(): whole = lax.psum(grads, 'dp')  34.4 us
    dot_general x9, matrix products, on_device(): jnp.einsum('hwo,io->hwi', grad_rows, kernel[a, b], preferred_element_type...  20.9 us
    dot_general x9, matrix products, on_device(): jnp.einsum('hwi,hwo->oi', xpad[a:a + count, b:b + width], grad_rows, pref...  12.2 us
    all_to_all x1, starting transfers between devices, pass_yards_on(): jax.lax.all_to_all(b_now, axis_name='filter', split_axis=0, concat_axis=0)  9.15 us
    reshape x1, local copies, waits for them, and re-layouts, on_device(): grads = jnp.stack(taps, 1).reshape(channels, 3, 3, local_in)  6.03 us
  transfers between devices with their start and end apart: 3, of which 2 were waited for; matrix products, arithmetic and copies ran while one was open for 47% of the time, Pallas kernels for 0%

profile of v1, /device:TPU:1, one launch (start us, length us, event | category | flops | bytes accessed | tf_op | source)
XLA Modules:
  0.0 225.6 jit_solution(15523568246439427183)
XLA Ops:
  8.0 2.7 %stack.41 = bf16[8,1,6,24,1024]{4,3,2,1,0:T(8,128)(2,1)} broadcast(bf16[6,24,1024]{2,1,0:T(8,128)(2,1)} %bitcast.200), dimensions={2,3,4} | broadcast | bytes 2654208 | tf_op jit(solution)/shard_map/stack | solution.py:9
  10.7 9.1 %all-to-all-start = ((bf16[8,1,6,24,1024]{4,3,2,1,0:T(8,128)(2,1)}), bf16[8,1,6,24,1024]{4,3,2,1,0:T(8,128)(2,1)S(1)}, u32[]{:S(2)}, u32[]{:S(2)}) async-start(bf16[8,1,6,24,1024]{4,3,2,1,0:T(8,128)(2,1)} %stack.41), calls=%async_computation.1 | async-start | bytes 4718592 | tf_op jit(solution)/shard_map/all_to_all | solution.py:10
  19.9 3.9 %fusion.15 = f32[48,24,1024]{2,1,0:T(8,128)} fusion(bf16[3,3,128,1024]{3,2,1,0:T(8,128)(2,1)} %param.4, bf16[48,24,128]{2,1,0:T(8,128)(2,1)S(1)} %bitcast.180), kind=kOutput, calls=%fused_computation.43 | convolution fusion | flops 301989888 | bytes 5275648 | tf_op jit(solution)/shard_map/hwi,io->hwo/dot_general | solution.py:18
  23.8 3.8 %fusion.18 = f32[48,24,1024]{2,1,0:T(8,128)} fusion(bf16[3,3,128,1024]{3,2,1,0:T(8,128)(2,1)} %param.4, bf16[48,24,128]{2,1,0:T(8,128)(2,1)S(1)} %bitcast.181), kind=kOutput, calls=%fused_computation.46 | convolution fusion | flops 301989888 | bytes 5275648 | tf_op jit(solution)/shard_map/hwi,io->hwo/dot_general | solution.py:18
  27.7 3.9 %fusion.21 = f32[48,24,1024]{2,1,0:T(8,128)} fusion(bf16[3,3,128,1024]{3,2,1,0:T(8,128)(2,1)} %param.4, bf16[48,24,128]{2,1,0:T(8,128)(2,1)S(1)} %bitcast.182), kind=kOutput, calls=%fused_computation.49 | convolution fusion | flops 301989888 | bytes 5275648 | tf_op jit(solution)/shard_map/hwi,io->hwo/dot_general | solution.py:18
  31.6 3.8 %fusion.27 = f32[48,24,1024]{2,1,0:T(8,128)} fusion(bf16[3,3,128,1024]{3,2,1,0:T(8,128)(2,1)} %param.4, bf16[48,24,128]{2,1,0:T(8,128)(2,1)S(1)} %bitcast.183), kind=kOutput, calls=%fused_computation.55 | convolution fusion | flops 301989888 | bytes 5275648 | tf_op jit(solution)/shard_map/hwi,io->hwo/dot_general | solution.py:18
  35.4 3.9 %fusion.30 = f32[48,24,1024]{2,1,0:T(8,128)} fusion(bf16[3,3,128,1024]{3,2,1,0:T(8,128)(2,1)} %param.4, bf16[48,24,128]{2,1,0:T(8,128)(2,1)S(1)} %bitcast.184), kind=kOutput, calls=%fused_computation.58 | convolution fusion | flops 301989888 | bytes 5275648 | tf_op jit(solution)/shard_map/hwi,io->hwo/dot_general | solution.py:18
  39.3 37.8 %all-to-all-done = bf16[8,1,6,24,1024]{4,3,2,1,0:T(8,128)(2,1)S(1)} async-done(((bf16[8,1,6,24,1024]{4,3,2,1,0:T(8,128)(2,1)}), bf16[8,1,6,24,1024]{4,3,2,1,0:T(8,128)(2,1)S(1)}, u32[]{:S(2)}, u32[]{:S(2)}) %all-to-all-start) | async-done | bytes 2359328 | tf_op jit(solution)/shard_map/all_to_all | solution.py:10
  82.6 1.4 fusion.6
  89.3 6.0 %copy.45 = f32[1024,3,3,128]{3,0,2,1:T(8,128)} copy(f32[1024,3,3,128]{0,3,2,1:T(8,128)} %bitcast.58) | data formatting | bytes 9437184 | tf_op jit(solution)/shard_map/reshape | solution.py:63
  95.5 4.2 %fusion.37 = f32[48,24,1024]{2,1,0:T(8,128)} fusion(bf16[3,3,128,1024]{3,2,1,0:T(8,128)(2,1)} %param.4, bf16[48,24,128]{2,1,0:T(8,128)(2,1)S(1)} %bitcast.193), kind=kOutput, calls=%fused_computation.65 | convolution fusion | flops 301989888 | bytes 5275648 | tf_op jit(solution)/shard_map/hwi,io->hwo/dot_general | solution.py:18
  99.7 4.0 %fusion.33 = f32[48,24,1024]{2,1,0:T(8,128)} fusion(bf16[3,3,128,1024]{3,2,1,0:T(8,128)(2,1)} %param.4, bf16[48,24,128]{2,1,0:T(8,128)(2,1)S(1)} %bitcast.194), kind=kOutput, calls=%fused_computation.61 | convolution fusion | flops 301989888 | bytes 5275648 | tf_op jit(solution)/shard_map/hwi,io->hwo/dot_general | solution.py:18
  103.7 3.9 %fusion.24 = f32[48,24,1024]{2,1,0:T(8,128)} fusion(bf16[3,3,128,1024]{3,2,1,0:T(8,128)(2,1)} %param.4, bf16[1,48,24,128]{3,2,1,0:T(8,128)(2,1)S(1)} %copy-done), kind=kOutput, calls=%fused_computation.52 | convolution fusion | flops 301989888 | bytes 5275648 | tf_op jit(solution)/shard_map/hwi,io->hwo/dot_general | solution.py:18
  107.7 13.1 %add_add_fusion = f32[48,24,1024]{2,1,0:T(8,128)} fusion(f32[48,24,1024]{2,1,0:T(8,128)S(1)} %bitcast.197, f32[48,24,1024]{2,1,0:T(8,128)S(1)} %bitcast.199, f32[48,24,1024]{2,1,0:T(8,128)} %fusion.21, f32[48,24,1024]{2,1,0:T(8,128)} %fusion.24, f32[48,24,1024]{2,1,0:T(8,128)} %fusion.27, f32[48,24,1024]{2,1,0:T(8,128)} %fusion.30, ...), kind=kOutput, calls=%fused_computation | convolution fusion | flops 311427072 | bytes 43024384 | tf_op jit(solution)/shard_map/hwi,io->hwo/dot_general | solution.py:18
  120.8 1.7 fusion.35
  122.7 2.6 %convolution_add_fusion.7 = f32[48,24,128]{2,1,0:T(8,128)} fusion(bf16[48,24,1024]{2,1,0:T(8,128)(2,1)S(1)} %bitcast.172, bf16[3,3,128,1024]{3,2,1,0:T(8,128)(2,1)} %param.4, f32[48,24,128]{2,1,0:T(8,128)S(1)} %fusion.35), kind=kOutput, calls=%fused_computation.10 | convolution fusion | flops 302137344 | bytes 3801088 | tf_op jit(solution)/shard_map/hwo,io->hwi/dot_general | solution.py:50
  125.2 6.4 %dynamic_update_slice.28 = f32[50,26,128]{2,1,0:T(8,128)S(1)} dynamic-update-slice(f32[50,26,128]{2,1,0:T(8,128)S(1)} %dynamic_update_slice.27, f32[48,24,128]{2,1,0:T(8,128)} %convolution_add_fusion.7, s32[]{:T(128)} %constant.5.clone.1, s32[]{:T(128)} %constant.6.clone.1, s32[]{:T(128)} %constant.5.clone.1) | dynamic-update-slice | bytes 1179652 | tf_op jit(solution)/shard_map/dynamic_update_slice | solution.py:54
  131.6 2.6 %convolution_add_fusion.6 = f32[48,24,128]{2,1,0:T(8,128)} fusion(bf16[48,24,1024]{2,1,0:T(8,128)(2,1)S(1)} %bitcast.173, f32[50,26,128]{2,1,0:T(8,128)S(1)} %dynamic_update_slice.28, bf16[3,3,128,1024]{3,2,1,0:T(8,128)(2,1)} %param.4), kind=kOutput, calls=%fused_computation.9 | convolution fusion | flops 302137344 | bytes 3801088 | tf_op jit(solution)/shard_map/hwo,io->hwi/dot_general | solution.py:50
  134.2 6.3 %dynamic_update_slice.29 = f32[50,26,128]{2,1,0:T(8,128)S(1)} dynamic-update-slice(f32[50,26,128]{2,1,0:T(8,128)S(1)} %dynamic_update_slice.28, f32[48,24,128]{2,1,0:T(8,128)} %convolution_add_fusion.6, s32[]{:T(128)} %constant.5.clone.1, s32[]{:T(128)} %constant.7.clone.1, s32[]{:T(128)} %constant.5.clone.1) | dynamic-update-slice | bytes 1179652 | tf_op jit(solution)/shard_map/dynamic_update_slice | solution.py:54
  140.5 1.9 fusion.1
  142.4 2.6 %convolution_add_fusion.4 = f32[48,24,128]{2,1,0:T(8,128)} fusion(bf16[48,24,1024]{2,1,0:T(8,128)(2,1)S(1)} %bitcast.175, f32[50,26,128]{2,1,0:T(8,128)S(1)} %fusion.1, bf16[3,3,128,1024]{3,2,1,0:T(8,128)(2,1)} %param.4), kind=kOutput, calls=%fused_computation.6 | convolution fusion | flops 302137344 | bytes 3801088 | tf_op jit(solution)/shard_map/hwo,io->hwi/dot_general | solution.py:50
  145.0 6.3 %dynamic_update_slice.31 = f32[50,26,128]{2,1,0:T(8,128)S(1)} dynamic-update-slice(f32[50,26,128]{2,1,0:T(8,128)S(1)} %fusion.1, f32[48,24,128]{2,1,0:T(8,128)} %convolution_add_fusion.4, s32[]{:T(128)} %constant.6.clone.1, s32[]{:T(128)} %constant.6.clone.1, s32[]{:T(128)} %constant.5.clone.1) | dynamic-update-slice | bytes 1179652 | tf_op jit(solution)/shard_map/dynamic_update_slice | solution.py:54
  151.2 2.6 %convolution_add_fusion.3 = f32[48,24,128]{2,1,0:T(8,128)} fusion(bf16[48,24,1024]{2,1,0:T(8,128)(2,1)S(1)} %bitcast.176, f32[50,26,128]{2,1,0:T(8,128)S(1)} %dynamic_update_slice.31, bf16[3,3,128,1024]{3,2,1,0:T(8,128)(2,1)} %param.4), kind=kOutput, calls=%fused_computation.5 | convolution fusion | flops 302137344 | bytes 3801088 | tf_op jit(solution)/shard_map/hwo,io->hwi/dot_general | solution.py:50
  153.8 6.3 %dynamic_update_slice.32 = f32[50,26,128]{2,1,0:T(8,128)S(1)} dynamic-update-slice(f32[50,26,128]{2,1,0:T(8,128)S(1)} %dynamic_update_slice.31, f32[48,24,128]{2,1,0:T(8,128)} %convolution_add_fusion.3, s32[]{:T(128)} %constant.6.clone.1, s32[]{:T(128)} %constant.7.clone.1, s32[]{:T(128)} %constant.5.clone.1) | dynamic-update-slice | bytes 1179652 | tf_op jit(solution)/shard_map/dynamic_update_slice | solution.py:54
  160.1 1.9 fusion
  162.0 2.6 %convolution_add_fusion.1 = f32[48,24,128]{2,1,0:T(8,128)} fusion(bf16[48,24,1024]{2,1,0:T(8,128)(2,1)S(1)} %bitcast.178, f32[50,26,128]{2,1,0:T(8,128)S(1)} %fusion, bf16[3,3,128,1024]{3,2,1,0:T(8,128)(2,1)} %param.4), kind=kOutput, calls=%fused_computation.2 | convolution fusion | flops 302137344 | bytes 3801088 | tf_op jit(solution)/shard_map/hwo,io->hwi/dot_general | solution.py:50
  164.5 6.2 %dynamic_update_slice.34 = f32[50,26,128]{2,1,0:T(8,128)S(1)} dynamic-update-slice(f32[50,26,128]{2,1,0:T(8,128)S(1)} %fusion, f32[48,24,128]{2,1,0:T(8,128)} %convolution_add_fusion.1, s32[]{:T(128)} %constant.7.clone.1, s32[]{:T(128)} %constant.6.clone.1, s32[]{:T(128)} %constant.5.clone.1) | dynamic-update-slice | bytes 1179652 | tf_op jit(solution)/shard_map/dynamic_update_slice | solution.py:54
  170.8 2.6 %convolution_add_fusion = f32[48,24,128]{2,1,0:T(8,128)} fusion(bf16[48,24,1024]{2,1,0:T(8,128)(2,1)S(1)} %bitcast.179, f32[50,26,128]{2,1,0:T(8,128)S(1)} %dynamic_update_slice.34, bf16[3,3,128,1024]{3,2,1,0:T(8,128)(2,1)} %param.4), kind=kOutput, calls=%fused_computation.1 | convolution fusion | flops 302137344 | bytes 3801088 | tf_op jit(solution)/shard_map/hwo,io->hwi/dot_general | solution.py:50
  173.3 6.2 %dynamic_update_slice.35 = f32[50,26,128]{2,1,0:T(8,128)S(1)} dynamic-update-slice(f32[50,26,128]{2,1,0:T(8,128)S(1)} %dynamic_update_slice.34, f32[48,24,128]{2,1,0:T(8,128)} %convolution_add_fusion, s32[]{:T(128)} %constant.7.clone.1, s32[]{:T(128)} %constant.7.clone.1, s32[]{:T(128)} %constant.5.clone.1) | dynamic-update-slice | bytes 1179652 | tf_op jit(solution)/shard_map/dynamic_update_slice | solution.py:54
  180.4 34.4 %all-reduce.4.cloned.1.call-done = f32[1024,3,3,128]{3,0,2,1:T(8,128)} async-done(((f32[1024,3,3,128]{3,0,2,1:T(8,128)}), f32[1024,3,3,128]{3,0,2,1:T(8,128)}) %all-reduce.4.cloned.1.call-update) | async-done | bytes 4718608 | tf_op jit(solution)/shard_map/psum | solution.py:68
  214.7 1.6 dynamic-slice_multiply_fusion
  216.3 1.8 convert_bitcast_fusion
  (27 shorter events, 11.8 us)
Async XLA Ops:
  10.7 9.2 %copy-start = (bf16[1,48,24,128]{3,2,1,0:T(8,128)(2,1)S(1)}, bf16[1,48,24,128]{3,2,1,0:T(8,128)(2,1)}, u32[]{:S(2)}) copy-start(bf16[1,48,24,128]{3,2,1,0:T(8,128)(2,1)} %param.3) | copy-start | bytes 884740
  10.7 66.4 %all-to-all-start = ((bf16[8,1,6,24,1024]{4,3,2,1,0:T(8,128)(2,1)}), bf16[8,1,6,24,1024]{4,3,2,1,0:T(8,128)(2,1)S(1)}, u32[]{:S(2)}, u32[]{:S(2)}) async-start(bf16[8,1,6,24,1024]{4,3,2,1,0:T(8,128)(2,1)} %stack.41), calls=%async_computation.1 | async-start | bytes 4718592 | tf_op jit(solution)/shard_map/all_to_all | solution.py:10
  19.9 194.9 %all-reduce.4.cloned.1.call-start = ((), (), s32[]{:S(2)}) async-start(), calls=%async_computation.3 | async-start | bytes 9437184 | tf_op jit(solution)/shard_map/psum | solution.py:68
  95.4 120.9 %reduce-scatter.2.cloned.1.call-start = ((), (), s32[]{:S(2)}) async-start(), calls=%async_computation.2 | async-start | bytes 5308416 | tf_op jit(solution)/shard_map/reduce_scatter | solution.py:36
  95.4 12.2 %slice-start = ((s8[4718592]{0:T(1024)(128)(4,1)}), s8[4194304]{0:T(1024)(128)(4,1)S(1)}, s32[]{:S(2)}) async-start(s8[4718592]{0:T(1024)(128)(4,1)} %bitcast.196), calls=%async_computation.4 | async-start | bytes 8388608
  95.5 12.2 %slice-start.2 = ((s8[4718592]{0:T(1024)(128)(4,1)}), s8[4194304]{0:T(1024)(128)(4,1)S(1)}, s32[]{:S(2)}) async-start(s8[4718592]{0:T(1024)(128)(4,1)} %bitcast.198), calls=%async_computation.6 | async-start | bytes 8388608
  99.7 8.0 %slice-start.1 = ((s8[4718592]{0:T(1024)(128)(4,1)}), s8[524288]{0:T(1024)(128)(4,1)S(1)}, s32[]{:S(2)}) async-start(s8[4718592]{0:T(1024)(128)(4,1)} %bitcast.196), calls=%async_computation.5 | async-start | bytes 1048576
  99.7 8.0 %slice-start.3 = ((s8[4718592]{0:T(1024)(128)(4,1)}), s8[524288]{0:T(1024)(128)(4,1)S(1)}, s32[]{:S(2)}) async-start(s8[4718592]{0:T(1024)(128)(4,1)} %bitcast.198), calls=%async_computation.7 | async-start | bytes 1048576
Sparse Core Ops, SparseCore 0:
  95.5 119.1 all-reduce.3
Sparse Core Ops, SparseCore 1:
  120.9 56.5 reduce-scatter.1
